TPU v7x, 32 devices: a whole 2x2x4 slice. The times are simulated.
32 devices in a mesh: dp: 16 (over z, y, x), mp: 2 (over core).
Axes of the slice: x: 2, y: 2, z: 4, core: 2. Of those that a mesh axis runs over, the one named last changes fastest.
Arguments:
- hidden: bfloat16 [2, 64, 64, 768], P(None, 'dp'), may hold values from -6 to 6
- encoder_tokens: bfloat16 [2, 32, 576, 768], P(None, 'dp'), may hold values from -6 to 6
- segment_ids: int32 [2, 64, 64], P(None, 'dp'), may hold values from 0 to 3, never falling along the last dimension, each value on 1 to 32 neighbouring positions
- image_index: int32 [2, 64], P(None, 'dp'), may hold values from 0 to 1
- cotangent: bfloat16 [2, 64, 64, 768], P(None, 'dp'), may hold values from -6 to 6
- norm_gains: bfloat16 [3, 768], P(None, 'dp'), may hold values from 0.099609375 to 1.8984375
- qkv_weight: bfloat16 [3, 768, 768], P(None, 'dp', 'mp'), may hold values from -0.21875 to 0.21875
- self_out_weight: bfloat16 [768, 768], P('dp', 'mp'), may hold values from -0.875 to 0.875
- cross_query_weight: bfloat16 [768, 768], P('dp', 'mp'), may hold values from -0.21875 to 0.21875
- cross_kv_weight: bfloat16 [2, 768, 768], P(None, 'dp', 'mp'), may hold values from -0.21875 to 0.21875
- cross_out_weight: bfloat16 [768, 768], P('dp', 'mp'), may hold values from -2.5 to 2.5
- up_weight: bfloat16 [768, 3072], P('dp', 'mp'), may hold values from -0.21875 to 0.21875
- down_weight: bfloat16 [768, 3072], P('dp', 'mp'), may hold values from -0.109375 to 0.109375
Outputs:
- output: bfloat16 [2, 64, 64, 768], P(None, 'dp')
- input_grad: float32 [2, 64, 64, 768], P(None, 'dp')
- encoder_grad: float32 [2, 32, 576, 768], P(None, 'dp', None, 'mp')
- grad_norm_gains: float32 [3, 768], P(None, 'dp')
- grad_qkv: float32 [3, 768, 768], P(None, 'dp', 'mp')
- grad_self_out: float32 [768, 768], P('dp', 'mp')
- grad_cross_query: float32 [768, 768], P('dp', 'mp')
- grad_cross_kv: float32 [2, 768, 768], P(None, 'dp', 'mp')
- grad_cross_out: float32 [768, 768], P('dp', 'mp')
- grad_up: float32 [768, 3072], P('dp', 'mp')
- grad_down: float32 [768, 3072], P('dp', 'mp')
Inputs may be any that keep to these rules, and one draw needn't show every extreme that they name: `segment_ids`: within a row the ids never fall; they number the 4 captions of the row, each of 1 to 32 tokens. Caption row r of a micro-batch reads image (r // 4) * 2 + image_index of that row.
All inputs are finite; a program needn't handle non-finite values.
Results may differ from a plain program's by a relative error of at most 0.019.
Values may be sent and summed in bfloat16 or wider, within the bound.
A program may use at most 192 MiB of HBM per device.

v0:
```python
import jax
import jax.numpy as jnp
from jax import lax
from jax.sharding import PartitionSpec as P

HEAD = 64
EPSILON = 1e-05
NEGATIVE = -1e30


def layer_norm(values, gain_row):
    centred = values - jnp.mean(values, axis=-1, keepdims=True)
    spread = jnp.mean(centred * centred, axis=-1, keepdims=True)
    return centred * lax.rsqrt(spread + EPSILON) * gain_row


def gelu_exact(values):
    return jax.nn.gelu(values, approximate=False)


def token_outer(left, right):
    return lax.dot_general(
        left, right, (((0,), (0,)), ((), ())), preferred_element_type=jnp.float32
    )


def feature_inner(left, right):
    return lax.dot_general(
        left, right, (((1,), (1,)), ((), ())), preferred_element_type=jnp.float32
    )


def attend(queries, key_heads, value_heads, allowed, score_scale):
    scores = (
        jnp.einsum("rqhe,rkhe->rhqk", queries, key_heads, preferred_element_type=jnp.float32)
        * score_scale
    )
    if allowed is not None:
        scores = jnp.where(allowed[:, None], scores, NEGATIVE)
    row_max = jnp.max(scores, axis=-1, keepdims=True)
    shifted = jnp.exp(scores - row_max)
    row_total = jnp.sum(shifted, axis=-1, keepdims=True)
    weights_low = (shifted / row_total).astype(jnp.bfloat16)
    mixed_heads = jnp.einsum(
        "rhqk,rkhe->rqhe", weights_low, value_heads, preferred_element_type=jnp.float32
    )
    return (mixed_heads.astype(jnp.bfloat16), row_max + jnp.log(row_total))


def attend_back(queries, key_heads, value_heads, allowed, score_scale, log_total, grad_mixed):
    scores = (
        jnp.einsum("rqhe,rkhe->rhqk", queries, key_heads, preferred_element_type=jnp.float32)
        * score_scale
    )
    if allowed is not None:
        scores = jnp.where(allowed[:, None], scores, NEGATIVE)
    probability = jnp.exp(scores - log_total)
    grad_weights = jnp.einsum(
        "rqhe,rkhe->rhqk", grad_mixed, value_heads, preferred_element_type=jnp.float32
    )
    inner_sum = jnp.sum(probability * grad_weights, axis=-1, keepdims=True)
    grad_scores = (probability * (grad_weights - inner_sum)).astype(jnp.bfloat16)
    grad_queries = (
        jnp.einsum("rhqk,rkhe->rqhe", grad_scores, key_heads, preferred_element_type=jnp.float32)
        * score_scale
    )
    grad_keys = (
        jnp.einsum("rhqk,rqhe->rkhe", grad_scores, queries, preferred_element_type=jnp.float32)
        * score_scale
    )
    grad_values = jnp.einsum(
        "rhqk,rqhe->rkhe",
        probability.astype(jnp.bfloat16),
        grad_mixed,
        preferred_element_type=jnp.float32,
    )
    return (grad_queries, grad_keys, grad_values)


def fetch_weights(
    norm_gains,
    qkv_weight,
    self_out_weight,
    cross_query_weight,
    cross_kv_weight,
    cross_out_weight,
    up_weight,
    down_weight,
):
    return (
        lax.all_gather(norm_gains, "dp", axis=1, tiled=True),
        lax.all_gather(qkv_weight, "dp", axis=1, tiled=True),
        lax.all_gather(self_out_weight, "dp", axis=0, tiled=True),
        lax.all_gather(cross_query_weight, "dp", axis=0, tiled=True),
        lax.all_gather(cross_kv_weight, "dp", axis=1, tiled=True),
        lax.all_gather(cross_out_weight, "dp", axis=0, tiled=True),
        lax.all_gather(up_weight, "dp", axis=0, tiled=True),
        lax.all_gather(down_weight, "dp", axis=0, tiled=True),
    )


def reduce_weight_grads(gradients):
    return (
        lax.psum_scatter(gradients[0], "dp", scatter_dimension=1, tiled=True),
        lax.psum_scatter(gradients[1], "dp", scatter_dimension=1, tiled=True),
        lax.psum_scatter(gradients[2], "dp", scatter_dimension=0, tiled=True),
        lax.psum_scatter(gradients[3], "dp", scatter_dimension=0, tiled=True),
        lax.psum_scatter(gradients[4], "dp", scatter_dimension=1, tiled=True),
        lax.psum_scatter(gradients[5], "dp", scatter_dimension=0, tiled=True),
        lax.psum_scatter(gradients[6], "dp", scatter_dimension=0, tiled=True),
        lax.psum_scatter(gradients[7], "dp", scatter_dimension=0, tiled=True),
    )


def branch_output(mixed_heads, weight):
    return lax.psum(feature_inner(mixed_heads, weight), "mp")


def input_grad_sum(partial_sum):
    return lax.psum(partial_sum.astype(jnp.bfloat16), "mp").astype(jnp.float32)


def add_pair(first, second):
    return first + second


def micro_step(gathered, hidden, encoder, segment, image_ids, cotangent):
    (
        norm_gains,
        qkv_weight,
        self_out_weight,
        cross_query_weight,
        cross_kv_weight,
        cross_out_weight,
        up_weight,
        down_weight,
    ) = gathered
    row_count, length, model_width = hidden.shape
    image_count, context = (encoder.shape[0], encoder.shape[1])
    head_count = qkv_weight.shape[2] // HEAD
    tokens = row_count * length
    head_shape = (row_count, length, head_count, HEAD)
    score_scale = HEAD ** (-0.5)
    gain_rows = norm_gains.astype(jnp.float32)
    positions = jnp.arange(length)
    causal = positions[None, :] <= positions[:, None]
    allowed = causal[None] & (segment[:, :, None] == segment[:, None, :])
    flat_in = hidden.reshape(tokens, model_width).astype(jnp.float32)
    low_one = layer_norm(flat_in, gain_rows[0]).astype(jnp.bfloat16)
    projected = jnp.einsum(
        "td,jde->jte", low_one, qkv_weight, preferred_element_type=jnp.float32
    ).astype(jnp.bfloat16)
    queries = projected[0].reshape(head_shape)
    key_heads = projected[1].reshape(head_shape)
    value_heads = projected[2].reshape(head_shape)
    self_mixed, self_total = attend(queries, key_heads, value_heads, allowed, score_scale)
    self_flat = self_mixed.reshape(tokens, -1)
    resid_one = flat_in + branch_output(self_flat, self_out_weight)
    low_two = layer_norm(resid_one, gain_rows[1]).astype(jnp.bfloat16)
    cross_queries = (
        jnp.dot(low_two, cross_query_weight, preferred_element_type=jnp.float32)
        .astype(jnp.bfloat16)
        .reshape(head_shape)
    )
    image_kv = jnp.einsum(
        "ncd,jde->jnce", encoder, cross_kv_weight, preferred_element_type=jnp.float32
    ).astype(jnp.bfloat16)
    row_kv = jnp.take(image_kv, image_ids, axis=1).reshape(2, row_count, context, head_count, HEAD)
    cross_mixed, cross_total = attend(cross_queries, row_kv[0], row_kv[1], None, score_scale)
    cross_flat = cross_mixed.reshape(tokens, -1)
    resid_two = resid_one + branch_output(cross_flat, cross_out_weight)
    low_three = layer_norm(resid_two, gain_rows[2]).astype(jnp.bfloat16)
    pre_act = jnp.dot(low_three, up_weight, preferred_element_type=jnp.float32)
    activated = gelu_exact(pre_act).astype(jnp.bfloat16)
    resid_three = resid_two + branch_output(activated, down_weight)
    output_rows = resid_three.astype(jnp.bfloat16).reshape(row_count, length, model_width)
    grad_low = cotangent.reshape(tokens, model_width)
    grad_down = token_outer(grad_low, activated)
    grad_act = jnp.dot(grad_low, down_weight, preferred_element_type=jnp.float32)
    gelu_back = jax.vjp(gelu_exact, pre_act)[1]
    grad_pre = gelu_back(grad_act)[0].astype(jnp.bfloat16)
    grad_up = token_outer(low_three, grad_pre)
    grad_normed = input_grad_sum(feature_inner(grad_pre, up_weight))
    norm_back = jax.vjp(layer_norm, resid_two, gain_rows[2])[1]
    grad_resid, grad_gain_three = norm_back(grad_normed)
    grad_two = grad_low.astype(jnp.float32) + grad_resid
    low_grad_two = grad_two.astype(jnp.bfloat16)
    grad_cross_out = token_outer(low_grad_two, cross_flat)
    grad_cross_mixed = (
        jnp.dot(low_grad_two, cross_out_weight, preferred_element_type=jnp.float32)
        .astype(jnp.bfloat16)
        .reshape(head_shape)
    )
    grad_cq, grad_ck, grad_cv = attend_back(
        cross_queries, row_kv[0], row_kv[1], None, score_scale, cross_total, grad_cross_mixed
    )
    low_cq = grad_cq.reshape(tokens, -1).astype(jnp.bfloat16)
    chooser = (image_ids[:, None] == jnp.arange(image_count)[None, :]).astype(jnp.float32)
    grad_rows_kv = jnp.stack([grad_ck, grad_cv]).reshape(2, row_count, context, -1)
    grad_image_kv = jnp.einsum(
        "ri,jrce->jice", chooser, grad_rows_kv, precision=lax.Precision.HIGHEST
    ).astype(jnp.bfloat16)
    grad_cross_query = token_outer(low_two, low_cq)
    grad_cross_kv = jnp.einsum(
        "ncd,jnce->jde", encoder, grad_image_kv, preferred_element_type=jnp.float32
    )
    encoder_part = jnp.einsum(
        "jnce,jde->ncd", grad_image_kv, cross_kv_weight, preferred_element_type=jnp.float32
    )
    encoder_grad = lax.psum_scatter(
        encoder_part.astype(jnp.bfloat16), "mp", scatter_dimension=2, tiled=True
    ).astype(jnp.float32)
    grad_normed = input_grad_sum(feature_inner(low_cq, cross_query_weight))
    norm_back = jax.vjp(layer_norm, resid_one, gain_rows[1])[1]
    grad_resid, grad_gain_two = norm_back(grad_normed)
    grad_one = grad_two + grad_resid
    low_grad_one = grad_one.astype(jnp.bfloat16)
    grad_self_out = token_outer(low_grad_one, self_flat)
    grad_self_mixed = (
        jnp.dot(low_grad_one, self_out_weight, preferred_element_type=jnp.float32)
        .astype(jnp.bfloat16)
        .reshape(head_shape)
    )
    grad_sq, grad_sk, grad_sv = attend_back(
        queries, key_heads, value_heads, allowed, score_scale, self_total, grad_self_mixed
    )
    grad_projected = (
        jnp.stack([grad_sq, grad_sk, grad_sv]).reshape(3, tokens, -1).astype(jnp.bfloat16)
    )
    grad_qkv = jnp.einsum(
        "td,jte->jde", low_one, grad_projected, preferred_element_type=jnp.float32
    )
    grad_normed = input_grad_sum(
        jnp.einsum("jte,jde->td", grad_projected, qkv_weight, preferred_element_type=jnp.float32)
    )
    norm_back = jax.vjp(layer_norm, flat_in, gain_rows[0])[1]
    grad_resid, grad_gain_one = norm_back(grad_normed)
    input_rows = (grad_one + grad_resid).reshape(row_count, length, model_width)
    grad_gains = jnp.stack([grad_gain_one, grad_gain_two, grad_gain_three])
    gradients = (
        grad_gains,
        grad_qkv,
        grad_self_out,
        grad_cross_query,
        grad_cross_kv,
        grad_cross_out,
        grad_up,
        grad_down,
    )
    return (output_rows, input_rows, encoder_grad, gradients)


def body(
    hidden,
    encoder_tokens,
    segment_ids,
    image_index,
    cotangent,
    norm_gains,
    qkv_weight,
    self_out_weight,
    cross_query_weight,
    cross_kv_weight,
    cross_out_weight,
    up_weight,
    down_weight,
):
    micro_count = hidden.shape[0]
    gathered = None
    outputs = []
    input_grads = []
    encoder_grads = []
    reduced = None
    for micro_index in range(micro_count):
        gathered = fetch_weights(
            norm_gains,
            qkv_weight,
            self_out_weight,
            cross_query_weight,
            cross_kv_weight,
            cross_out_weight,
            up_weight,
            down_weight,
        )
        output_rows, input_rows, encoder_rows, gradients = micro_step(
            gathered,
            hidden[micro_index],
            encoder_tokens[micro_index],
            segment_ids[micro_index],
            image_index[micro_index],
            cotangent[micro_index],
        )
        outputs.append(output_rows)
        input_grads.append(input_rows)
        encoder_grads.append(encoder_rows)
        shards = reduce_weight_grads(gradients)
        reduced = shards if reduced is None else jax.tree.map(add_pair, reduced, shards)
    return (
        jnp.stack(outputs),
        jnp.stack(input_grads),
        jnp.stack(encoder_grads),
        reduced[0],
        reduced[1],
        reduced[2],
        reduced[3],
        reduced[4],
        reduced[5],
        reduced[6],
        reduced[7],
    )


def solution(mesh):
    placed = (
        P(None, "dp", None, None),
        P(None, "dp", None, None),
        P(None, "dp", None),
        P(None, "dp"),
        P(None, "dp", None, None),
        P(None, "dp"),
        P(None, "dp", "mp"),
        P("dp", "mp"),
        P("dp", "mp"),
        P(None, "dp", "mp"),
        P("dp", "mp"),
        P("dp", "mp"),
        P("dp", "mp"),
    )
    return jax.shard_map(
        body,
        mesh=mesh,
        in_specs=placed,
        out_specs=(
            P(None, "dp", None, None),
            P(None, "dp", None, None),
            P(None, "dp", None, "mp"),
            P(None, "dp"),
            P(None, "dp", "mp"),
            P("dp", "mp"),
            P("dp", "mp"),
            P(None, "dp", "mp"),
            P("dp", "mp"),
            P("dp", "mp"),
            P("dp", "mp"),
        ),
        check_vma=False,
    )
```

profile of v0, /device:TPU:0, one launch (start us, length us, event | category | flops | bytes accessed | tf_op | source)
XLA Modules:
  0.0 1708.3 jit_solution(6245522283395078489)
XLA Ops:
  11.9 42.4 %all-gather = bf16[16,48,3]{1,2,0:T(4,128)(2,1)S(1)} all-gather(bf16[1,48,3]{1,2,0:T(4,128)(2,1)S(1)} %bitcast.350), channel_id=1, replica_groups=mesh['dp'=16,'mp'=2] {'dp'}, dimensions={0}, use_global_device_ids=true | all-gather | bytes 4896 | tf_op jit(solution)/shard_map/all_gather | solution.py:91
  56.9 40.3 %all_gather.34 = bf16[768,384]{1,0:T(8,128)(2,1)S(1)} all-gather(bf16[48,384]{1,0:T(8,128)(2,1)S(1)} %copy-done.100), channel_id=1, replica_groups=mesh['dp'=16,'mp'=2] {'dp'}, dimensions={0}, use_global_device_ids=true | all-gather | bytes 626688 | tf_op jit(solution)/shard_map/all_gather | solution.py:93
  97.3 44.4 %all_gather.36 = bf16[768,384]{1,0:T(8,128)(2,1)} all-gather(bf16[48,384]{1,0:T(8,128)(2,1)S(1)} %copy-done.101), channel_id=1, replica_groups=mesh['dp'=16,'mp'=2] {'dp'}, dimensions={0}, use_global_device_ids=true | all-gather | bytes 626688 | tf_op jit(solution)/shard_map/all_gather | solution.py:94
  141.7 40.7 %all_gather.37 = bf16[768,384]{1,0:T(8,128)(2,1)S(1)} all-gather(bf16[48,384]{1,0:T(8,128)(2,1)S(1)} %copy-done.102), channel_id=1, replica_groups=mesh['dp'=16,'mp'=2] {'dp'}, dimensions={0}, use_global_device_ids=true | all-gather | bytes 626688 | tf_op jit(solution)/shard_map/all_gather | solution.py:96
  182.4 4.8 convert_bitcast_fusion
  187.2 4.3 gather_fusion.1
  214.5 2.8 select_bitcast_fusion
  219.5 4.0 copy.281
  223.5 4.2 convert_bitcast_fusion.1
  227.7 4.4 gather_fusion
  232.2 2.5 select_bitcast_fusion.1
  236.8 3.9 copy.268
  240.7 3.9 copy.266
  244.6 3.9 copy.279
  257.7 2.5 multiply_reduce_fusion.3
  281.2 14.4 all-reduce.21.cloned.1.call-done
  300.1 61.7 %all-gather.10.cloned.1.call-done = bf16[768,1536]{1,0:T(8,128)(2,1)} async-done(((bf16[48,1536]{1,0:T(8,128)(2,1)}), bf16[768,1536]{1,0:T(8,128)(2,1)}) %all-gather.10.cloned.1.call-update) | async-done | bytes 2359312 | tf_op jit(solution)/shard_map/all_gather | solution.py:97
  361.8 3.9 fusion.192
  365.7 59.9 %all-gather.12.cloned.1.call-done = bf16[768,1536]{1,0:T(8,128)(2,1)} async-done(((bf16[48,1536]{1,0:T(8,128)(2,1)}), bf16[768,1536]{1,0:T(8,128)(2,1)}) %all-gather.12.cloned.1.call-update) | async-done | bytes 2359312 | tf_op jit(solution)/shard_map/all_gather | solution.py:98
  425.6 6.4 add_convert_fusion
  437.4 5.1 add_convert_fusion.1
  445.1 3.8 fusion.213
  456.9 6.3 all-reduce.29.cloned.1.call-done
  463.3 2.7 fusion.119
  468.4 19.6 %all-reduce.19.cloned.1.call-done = (f32[256,768]{1,0:T(8,128)}, f32[256,768]{1,0:T(8,128)}) async-done(((f32[256,768]{1,0:T(8,128)}, f32[256,768]{1,0:T(8,128)}), (f32[256,768]{1,0:T(8,128)}, f32[256,768]{1,0:T(8,128)})) %all-reduce.19.cloned.1.call-update) | async-done | bytes 1572880 | tf_op jit(solution)/shard_map/psum | solution.py:116
  488.0 3.6 fusion.193
  506.9 4.5 multiply_reduce_fusion.1
  521.5 4.5 multiply_reduce_fusion
  541.5 5.1 fusion.27
  546.6 6.3 copy.329
  552.9 3.9 all-reduce.27.cloned.1.call-done
  558.8 2.5 fusion.120
  618.4 4.3 convolution_multiply_fusion.1
  622.6 6.2 copy.328
  628.8 10.9 fusion.16
  649.2 4.7 bitcast_convert_fusion.1
  653.9 6.6 copy.374
  660.4 5.0 reshape.449
  665.6 5.0 fusion.25
  670.6 6.1 copy.334
  676.7 4.2 convolution_multiply_fusion
  681.0 6.2 copy.333
  687.1 10.1 fusion.19
  698.5 2.8 bitcast_convert_fusion
  701.3 6.6 copy.376
  707.8 5.0 reshape.451
  713.1 3.9 fusion.35
  717.1 3.2 fusion.24
  720.3 5.3 copy.341
  727.6 2.5 add_bitcast_fusion.1
  730.1 6.2 copy.338
  748.6 3.1 convolution_add_fusion
  754.1 3.0 add_bitcast_fusion
  757.0 6.1 copy.380
  773.5 9.2 reduce-scatter.25.cloned.1.call-done
  782.7 2.7 reshape.450
  787.2 8.2 reduce-scatter.27.cloned.1.call-done
  795.4 2.7 reshape.452
  801.9 229.5 %all-reduce.17.cloned.1.call-done = (f32[3,768,384]{2,0,1:T(4,128)}, f32[2,768,384]{2,0,1:T(2,128)}) async-done(((f32[3,768,384]{2,0,1:T(4,128)}, f32[2,768,384]{2,0,1:T(2,128)}), (f32[3,768,384]{2,0,1:T(4,128)}, f32[2,768,384]{2,0,1:T(2,128)})) %all-reduce.17.cloned.1.call-update) | async-done | bytes 5898256
  1034.8 125.2 %reduce-scatter.21.cloned.1.call-done = f32[48,384]{1,0:T(8,128)} async-done(((f32[768,384]{1,0:T(8,128)}), f32[48,384]{1,0:T(8,128)}) %reduce-scatter.21.cloned.1.call-update) | async-done | bytes 73744 | tf_op jit(solution)/shard_map/reduce_scatter | solution.py:109
  1159.9 128.6 %reduce-scatter.19.cloned.1.call-done = f32[48,384]{1,0:T(8,128)} async-done(((f32[768,384]{1,0:T(8,128)}), f32[48,384]{1,0:T(8,128)}) %reduce-scatter.19.cloned.1.call-update) | async-done | bytes 73744 | tf_op jit(solution)/shard_map/reduce_scatter | solution.py:107
  1288.5 128.5 %reduce-scatter.17.cloned.1.call-done = f32[48,384]{1,0:T(8,128)} async-done(((f32[768,384]{1,0:T(8,128)}), f32[48,384]{1,0:T(8,128)}) %reduce-scatter.17.cloned.1.call-update) | async-done | bytes 73744 | tf_op jit(solution)/shard_map/reduce_scatter | solution.py:106
  1417.0 142.4 %reduce-scatter.23.cloned.1.call-done = f32[48,1536]{1,0:T(8,128)} async-done(((f32[768,1536]{1,0:T(8,128)}), f32[48,1536]{1,0:T(8,128)}) %reduce-scatter.23.cloned.1.call-update) | async-done | bytes 294928 | tf_op jit(solution)/shard_map/reduce_scatter | solution.py:110
  1559.5 141.9 %reduce-scatter.31.cloned.1.call-done = f32[48,1536]{1,0:T(8,128)} async-done(((f32[768,1536]{1,0:T(8,128)}), f32[48,1536]{1,0:T(8,128)}) %reduce-scatter.31.cloned.1.call-update) | async-done | bytes 294928
  (522 shorter events, 232.3 us)
Async XLA Ops:
  7.2 48.7 %copy-start.4 = (bf16[2,4,64,768]{3,2,1,0:T(8,128)(2,1)S(1)}, bf16[2,4,64,768]{3,2,1,0:T(8,128)(2,1)}, u32[]{:S(2)}) copy-start(bf16[2,4,64,768]{3,2,1,0:T(8,128)(2,1)} %param.15) | copy-start | bytes 2359300
  7.2 4.8 copy-start.134
  7.2 47.3 %copy-start.130 = (s32[2,4]{1,0:T(2,128)S(1)}, s32[2,4]{1,0:T(2,128)}, u32[]{:S(2)}) copy-start(s32[2,4]{1,0:T(2,128)} %param.18) | copy-start | bytes 100
  7.2 47.9 %copy-start.131 = (s32[2,4,64]{2,1,0:T(4,128)S(1)}, s32[2,4,64]{2,1,0:T(4,128)}, u32[]{:S(2)}) copy-start(s32[2,4,64]{2,1,0:T(4,128)} %param.17) | copy-start | bytes 6148
  7.2 175.2 %all-gather.8.cloned.1.call-start = ((), (), s32[]{:S(2)}) async-start(), calls=%async_computation.9 | async-start | bytes 1253376 | tf_op jit(solution)/shard_map/all_gather | solution.py:95
  8.0 49.0 %copy-start.100 = (bf16[48,384]{1,0:T(8,128)(2,1)S(1)}, bf16[48,384]{1,0:T(8,128)(2,1)}, u32[]{:S(2)}) copy-start(bf16[48,384]{1,0:T(8,128)(2,1)} %param.22) | copy-start | bytes 110596
  8.0 183.6 %all-gather.6.cloned.1.call-start = ((), (), s32[]{:S(2)}) async-start(), calls=%async_computation.8 | async-start | bytes 1880064 | tf_op jit(solution)/shard_map/all_gather | solution.py:92
  8.7 239.7 %all-reduce.23.cloned.1.call-start = ((), (), s32[]{:S(2)}) async-start(), calls=%async_computation.23 | async-start | bytes 3145728 | tf_op jit(solution)/shard_map/psum | solution.py:116
  10.1 87.2 %copy-start.101 = (bf16[48,384]{1,0:T(8,128)(2,1)S(1)}, bf16[48,384]{1,0:T(8,128)(2,1)}, u32[]{:S(2)}) copy-start(bf16[48,384]{1,0:T(8,128)(2,1)} %param.23) | copy-start | bytes 110596
  10.1 131.6 %copy-start.102 = (bf16[48,384]{1,0:T(8,128)(2,1)S(1)}, bf16[48,384]{1,0:T(8,128)(2,1)}, u32[]{:S(2)}) copy-start(bf16[48,384]{1,0:T(8,128)(2,1)} %param.25) | copy-start | bytes 110596
  11.7 170.7 %copy-start.107 = (f32[256]{0:T(256)}, f32[256]{0:T(256)S(1)}, u32[]{:S(2)}) copy-start(f32[256]{0:T(256)S(1)} %div.157) | copy-start | bytes 3076
  11.7 170.6 %copy-start.109 = (f32[256]{0:T(256)}, f32[256]{0:T(256)S(1)}, u32[]{:S(2)}) copy-start(f32[256]{0:T(256)S(1)} %div.168) | copy-start | bytes 3076
  11.8 43.2 %copy-start.123 = (f32[256]{0:T(256)}, f32[256]{0:T(256)S(1)}, u32[]{:S(2)}) copy-start(f32[256]{0:T(256)S(1)} %add.228) | copy-start | bytes 3076
  11.8 170.5 %copy-start.113 = (f32[256]{0:T(256)}, f32[256]{0:T(256)S(1)}, u32[]{:S(2)}) copy-start(f32[256]{0:T(256)S(1)} %rsqrt.66) | copy-start | bytes 3076
  11.9 43.1 %copy-start.124 = (f32[256]{0:T(256)}, f32[256]{0:T(256)S(1)}, u32[]{:S(2)}) copy-start(f32[256]{0:T(256)S(1)} %add.235) | copy-start | bytes 3076
  11.9 170.4 %copy-start.115 = (f32[256]{0:T(256)}, f32[256]{0:T(256)S(1)}, u32[]{:S(2)}) copy-start(f32[256]{0:T(256)S(1)} %rsqrt.69) | copy-start | bytes 3076
  56.9 134.6 %copy-start.67 = (bf16[256,768]{1,0:T(8,128)(2,1)}, bf16[256,768]{1,0:T(8,128)(2,1)S(1)}, u32[]{:S(2)}) copy-start(bf16[256,768]{1,0:T(8,128)(2,1)S(1)} %get-tuple-element.120) | copy-start | bytes 1179652
  97.3 115.6 %copy-start.15 = (bf16[768,384]{1,0:T(8,128)(2,1)}, bf16[768,384]{1,0:T(8,128)(2,1)S(1)}, u32[]{:S(2)}) copy-start(bf16[768,384]{1,0:T(8,128)(2,1)S(1)} %all_gather.34) | copy-start | bytes 1769476
  182.4 95.4 %copy-start.18 = (bf16[768,384]{1,0:T(8,128)(2,1)}, bf16[768,384]{1,0:T(8,128)(2,1)S(1)}, u32[]{:S(2)}) copy-start(bf16[768,384]{1,0:T(8,128)(2,1)S(1)} %all_gather.37) | copy-start | bytes 1769476
  195.5 12.4 copy-start.43
  207.9 5.0 copy-start.58
  214.2 81.4 %all-reduce.21.cloned.1.call-start = ((), (), s32[]{:S(2)}) async-start(), calls=%async_computation.22 | async-start | bytes 3145728 | tf_op jit(solution)/shard_map/psum | solution.py:116
  227.7 4.4 copy-start.132
  254.6 12.4 copy-start.40
  266.9 9.6 copy-start.61
  279.1 82.6 %all-gather.10.cloned.1.call-start = ((), (), s32[]{:S(2)}) async-start(), calls=%async_computation.10 | async-start | bytes 2506752 | tf_op jit(solution)/shard_map/all_gather | solution.py:97
  279.7 145.8 %all-gather.12.cloned.1.call-start = ((), (), s32[]{:S(2)}) async-start(), calls=%async_computation.11 | async-start | bytes 2506752 | tf_op jit(solution)/shard_map/all_gather | solution.py:98
  280.3 183.0 %all-reduce.29.cloned.1.call-start = ((), (), s32[]{:S(2)}) async-start(), calls=%async_computation.26 | async-start | bytes 1572864 | tf_op jit(solution)/shard_map/psum | solution.py:120
  425.6 6.4 copy-start.34
  445.0 43.0 %all-reduce.19.cloned.1.call-start = ((), (), s32[]{:S(2)}) async-start(), calls=%async_computation.21 | async-start | bytes 3145728 | tf_op jit(solution)/shard_map/psum | solution.py:116
  452.7 104.1 %all-reduce.27.cloned.1.call-start = ((), (), s32[]{:S(2)}) async-start(), calls=%async_computation.25 | async-start | bytes 1572864 | tf_op jit(solution)/shard_map/psum | solution.py:120
  488.0 4.5 copy-start.35
  488.0 5.5 copy-start.19
  506.9 4.5 copy-start.3
  506.9 4.5 copy-start.80
  521.5 4.5 copy-start.1
  521.5 4.5 copy-start.79
  536.2 104.7 %all-reduce.25.cloned.1.call-start = ((), (), s32[]{:S(2)}) async-start(), calls=%async_computation.24 | async-start | bytes 1572864 | tf_op jit(solution)/shard_map/psum | solution.py:120
  556.8 4.6 copy-start.119
  556.8 4.6 copy-start.49
  556.8 4.6 copy-start.99
  556.8 4.6 copy-start.106
  609.7 5.2 copy-start.78
  609.7 5.2 copy-start.138
  617.9 154.1 %reduce-scatter.29.cloned.1.call-start = ((), (), s32[]{:S(2)}) async-start(), calls=%async_computation.18 | async-start | bytes 417792
  628.8 10.9 copy-start.111
  628.8 11.5 copy-start.112
  640.9 5.3 copy-start.116
  640.9 5.3 copy-start.117
  649.1 133.5 %reduce-scatter.25.cloned.1.call-start = ((), (), s32[]{:S(2)}) async-start(), calls=%async_computation.16 | async-start | bytes 2654208
  665.4 130.0 %reduce-scatter.27.cloned.1.call-start = ((), (), s32[]{:S(2)}) async-start(), calls=%async_computation.17 | async-start | bytes 2654208
  687.1 11.3 copy-start.140
  712.8 318.6 %all-reduce.17.cloned.1.call-start = ((), (), s32[]{:S(2)}) async-start(), calls=%async_computation.20 | async-start | bytes 14155776
  736.4 423.6 %reduce-scatter.21.cloned.1.call-start = ((), (), s32[]{:S(2)}) async-start(), calls=%async_computation.14 | async-start | bytes 1253376 | tf_op jit(solution)/shard_map/reduce_scatter | solution.py:109
  739.4 549.1 %reduce-scatter.19.cloned.1.call-start = ((), (), s32[]{:S(2)}) async-start(), calls=%async_computation.13 | async-start | bytes 1253376 | tf_op jit(solution)/shard_map/reduce_scatter | solution.py:107
  743.4 673.6 %reduce-scatter.17.cloned.1.call-start = ((), (), s32[]{:S(2)}) async-start(), calls=%async_computation.12 | async-start | bytes 1253376 | tf_op jit(solution)/shard_map/reduce_scatter | solution.py:106
  746.4 813.1 %reduce-scatter.23.cloned.1.call-start = ((), (), s32[]{:S(2)}) async-start(), calls=%async_computation.15 | async-start | bytes 5013504 | tf_op jit(solution)/shard_map/reduce_scatter | solution.py:110
  751.8 949.5 %reduce-scatter.31.cloned.1.call-start = ((), (), s32[]{:S(2)}) async-start(), calls=%async_computation.19 | async-start | bytes 5013504
  763.1 5.4 copy-start.108
  763.1 5.4 copy-start.110
  763.1 5.4 copy-start.114
  763.1 5.4 copy-start.25
  763.2 5.4 copy-start.54
  763.2 5.4 copy-start.56
  (98 other events, 201.9 us)
Sparse Core Ops, SparseCore 0:
  10.7 59.4 all-gather.7
  72.9 61.2 all-gather.5
  214.3 16.3 all-reduce.22
  279.2 16.3 all-reduce.20
  298.3 63.4 all-gather.9
  364.4 61.0 all-gather.11
  445.1 18.0 all-reduce.28
  466.3 21.6 all-reduce.18
  536.3 20.4 all-reduce.26
  618.0 20.4 all-reduce.24
  649.3 122.7 reduce-scatter.28
  774.3 8.3 reduce-scatter.24
  784.9 10.4 reduce-scatter.26
  802.8 228.5 all-reduce.16
  1037.3 122.5 reduce-scatter.20
  1165.8 122.6 reduce-scatter.18
  1294.4 122.5 reduce-scatter.16
  1423.4 135.9 reduce-scatter.22
  1565.2 136.0 reduce-scatter.30
where the time goes:
time: 1720 us; the launch traced here: 1710 us
  waiting for transfers between devices  1080 us (63%)
  local copies, waits for them, and re-layouts  209 us (12%)
  matrix products  169 us (10%)
  blocking collectives  168 us (10%)
  other arithmetic  59.6 us (3%)
    unnamed x24, waiting for transfers between devices  392 us
    reduce_scatter x1, waiting for transfers between devices, reduce_weight_grads(): lax.psum_scatter(gradients[6], 'dp', scatter_dimension=0, tiled=True)  142 us
    reduce_scatter x1, waiting for transfers between devices, reduce_weight_grads(): lax.psum_scatter(gradients[3], 'dp', scatter_dimension=0, tiled=True)  129 us
    reduce_scatter x1, waiting for transfers between devices, reduce_weight_grads(): lax.psum_scatter(gradients[2], 'dp', scatter_dimension=0, tiled=True)  128 us
    reduce_scatter x1, waiting for transfers between devices, reduce_weight_grads(): lax.psum_scatter(gradients[5], 'dp', scatter_dimension=0, tiled=True)  125 us
    unnamed x306, local copies, waits for them, and re-layouts  68.8 us
    all_gather x1, waiting for transfers between devices, fetch_weights(): lax.all_gather(up_weight, 'dp', axis=0, tiled=True)  61.7 us
    all_gather x1, waiting for transfers between devices, fetch_weights(): lax.all_gather(down_weight, 'dp', axis=0, tiled=True)  59.9 us
  transfers between devices with their start and end apart: 19, of which 15 were waited for; matrix products, arithmetic and copies ran while one was open for 14% of the time, Pallas kernels for 0%

commit v1 on v0

--- a/solution.py
+++ b/solution.py
@@ -6,6 +6,27 @@
 HEAD = 64
 EPSILON = 1e-05
 NEGATIVE = -1e30
+
+
+def gather_around(shard, axis, dim):
+    peers, index, rows = (lax.axis_size(axis), lax.axis_index(axis), shard.shape[dim])
+    right = [(i, (i + 1) % peers) for i in range(peers)]
+    behind = [(i, (i - 1) % peers) for i in range(peers)]
+    result = jnp.zeros((*shard.shape[:dim], peers * rows, *shard.shape[dim + 1 :]), shard.dtype)
+    result = lax.dynamic_update_slice_in_dim(result, shard, index * rows, axis=dim)
+    from_left = from_right = shard
+    half = peers // 2
+    for step in range(1, half + 1):
+        from_left = lax.ppermute(from_left, axis, right)
+        result = lax.dynamic_update_slice_in_dim(
+            result, from_left, (index - step) % peers * rows, axis=dim
+        )
+        if step < peers - half:
+            from_right = lax.ppermute(from_right, axis, behind)
+            result = lax.dynamic_update_slice_in_dim(
+                result, from_right, (index + step) % peers * rows, axis=dim
+            )
+    return result
 
 
 def layer_norm(values, gain_row):
@@ -94,7 +115,7 @@
         lax.all_gather(cross_query_weight, "dp", axis=0, tiled=True),
         lax.all_gather(cross_kv_weight, "dp", axis=1, tiled=True),
         lax.all_gather(cross_out_weight, "dp", axis=0, tiled=True),
-        lax.all_gather(up_weight, "dp", axis=0, tiled=True),
+        gather_around(up_weight, "dp", 0),
         lax.all_gather(down_weight, "dp", axis=0, tiled=True),
     )
 

time: 1720 us -> 1670 us (0.971)
  waiting for transfers between devices: 1080 us -> 973 us
  starting transfers between devices: 2.2 us -> 39.5 us
    all_gather x1 -> x0, waiting for transfers between devices: 61.7 us -> none  [fetch_weights(): lax.all_gather(up_weight, 'dp', axis=0, tiled=True)]
    all_gather x1, waiting for transfers between devices: 59.9 us -> 0.01 us  [fetch_weights(): lax.all_gather(down_weight, 'dp', axis=0, tiled=True)]
    ppermute x0 -> x15, starting transfers between devices: none -> 37.5 us  [the longest x7 36.9 us: gather_around(): from_right = lax.ppermute(from_right, axis, behind)]
    ppermute x0 -> x15, waiting for transfers between devices: none -> 30.3 us  [the longest x8 23 us: gather_around(): from_left = lax.ppermute(from_left, axis, right)]
    unnamed x306 -> x302, local copies, waits for them, and re-layouts: 68.8 us -> 66.5 us
    unnamed x24 -> x23, waiting for transfers between devices: 392 us -> 391 us
  transfers between devices with their start and end apart: 19 -> 33, of which waited for: 15 -> 24; matrix products, arithmetic and copies ran while one was open for 14% -> 16% of each run, Pallas kernels for 0% -> 0%
where the time goes in v1:
time: 1670 us; the launch traced here: 1660 us
  waiting for transfers between devices  973 us (58%)
  local copies, waits for them, and re-layouts  225 us (13%)
  matrix products  177 us (11%)
  blocking collectives  165 us (10%)
  other arithmetic  58.2 us (3%)
  starting transfers between devices  39.5 us (2%)
  between operations  17.5 us (1%)
    unnamed x23, waiting for transfers between devices  391 us
    reduce_scatter x1, waiting for transfers between devices, reduce_weight_grads(): lax.psum_scatter(gradients[6], 'dp', scatter_dimension=0, tiled=True)  143 us
    reduce_scatter x1, waiting for transfers between devices, reduce_weight_grads(): lax.psum_scatter(gradients[2], 'dp', scatter_dimension=0, tiled=True)  129 us
    reduce_scatter x1, waiting for transfers between devices, reduce_weight_grads(): lax.psum_scatter(gradients[3], 'dp', scatter_dimension=0, tiled=True)  129 us
    reduce_scatter x1, waiting for transfers between devices, reduce_weight_grads(): lax.psum_scatter(gradients[5], 'dp', scatter_dimension=0, tiled=True)  125 us
    unnamed x302, local copies, waits for them, and re-layouts  66.5 us
    all_gather x1, blocking collectives, fetch_weights(): lax.all_gather(cross_query_weight, 'dp', axis=0, tiled=True)  42.9 us
    all_gather x1, blocking collectives, fetch_weights(): lax.all_gather(norm_gains, 'dp', axis=1, tiled=True)  42.4 us
  transfers between devices with their start and end apart: 33, of which 24 were waited for; matrix products, arithmetic and copies ran while one was open for 16% of the time, Pallas kernels for 0%

profile of v1, /device:TPU:0, one launch (start us, length us, event | category | flops | bytes accessed | tf_op | source)
XLA Modules:
  0.0 1656.7 jit_solution(173063561199506076)
XLA Ops:
  11.9 42.4 %all-gather = bf16[16,48,3]{1,2,0:T(4,128)(2,1)S(1)} all-gather(bf16[1,48,3]{1,2,0:T(4,128)(2,1)S(1)} %bitcast.350), channel_id=1, replica_groups=mesh['dp'=16,'mp'=2] {'dp'}, dimensions={0}, use_global_device_ids=true | all-gather | bytes 4896 | tf_op jit(solution)/shard_map/all_gather | solution.py:112
  56.9 40.3 %all_gather.30 = bf16[768,384]{1,0:T(8,128)(2,1)S(1)} all-gather(bf16[48,384]{1,0:T(8,128)(2,1)S(1)} %copy-done.98), channel_id=1, replica_groups=mesh['dp'=16,'mp'=2] {'dp'}, dimensions={0}, use_global_device_ids=true | all-gather | bytes 626688 | tf_op jit(solution)/shard_map/all_gather | solution.py:114
  97.3 42.9 %all_gather.32 = bf16[768,384]{1,0:T(8,128)(2,1)S(1)} all-gather(bf16[48,384]{1,0:T(8,128)(2,1)S(1)} %copy-done.99), channel_id=1, replica_groups=mesh['dp'=16,'mp'=2] {'dp'}, dimensions={0}, use_global_device_ids=true | all-gather | bytes 626688 | tf_op jit(solution)/shard_map/all_gather | solution.py:115
  140.2 39.6 %all_gather.33 = bf16[768,384]{1,0:T(8,128)(2,1)S(1)} all-gather(bf16[48,384]{1,0:T(8,128)(2,1)S(1)} %copy-done.100), channel_id=1, replica_groups=mesh['dp'=16,'mp'=2] {'dp'}, dimensions={0}, use_global_device_ids=true | all-gather | bytes 626688 | tf_op jit(solution)/shard_map/all_gather | solution.py:117
  179.9 4.8 convert_bitcast_fusion
  184.7 4.3 gather_fusion.1
  219.3 4.0 copy.281
  223.3 4.2 convert_bitcast_fusion.1
  227.5 4.5 gather_fusion
  236.7 3.9 copy.268
  240.6 3.9 copy.266
  244.5 3.9 copy.279
  289.2 4.7 collective-permute-start.3
  296.6 6.2 collective-permute-start.5
  306.7 6.1 collective-permute-start.7
  316.8 6.1 collective-permute-start.9
  325.6 6.2 collective-permute-start.11
  335.3 6.1 collective-permute-start.13
  345.1 7.4 collective-permute-done.12
  353.9 10.5 collective-permute-done.14
  368.1 3.7 fusion.191
  371.7 3.6 fusion.192
  375.4 6.4 add_convert_fusion
  383.0 3.4 convolution_convert_fusion.2
  386.4 5.3 add_convert_fusion.1
  392.5 3.2 convolution_convert_fusion.3
  395.9 3.9 fusion.213
  407.5 3.6 all-reduce.29.cloned.1.call-done
  416.3 19.6 %all-reduce.19.cloned.1.call-done = (f32[256,768]{1,0:T(8,128)}, f32[256,768]{1,0:T(8,128)}) async-done(((f32[256,768]{1,0:T(8,128)}, f32[256,768]{1,0:T(8,128)}), (f32[256,768]{1,0:T(8,128)}, f32[256,768]{1,0:T(8,128)})) %all-reduce.19.cloned.1.call-update) | async-done | bytes 1572880 | tf_op jit(solution)/shard_map/psum | solution.py:137
  435.9 3.7 fusion.193
  454.8 4.5 multiply_reduce_fusion.1
  469.4 4.5 multiply_reduce_fusion
  489.3 5.1 fusion.27
  494.5 6.3 copy.329
  500.8 3.9 all-reduce.27.cloned.1.call-done
  566.4 4.3 convolution_multiply_fusion.1
  570.7 6.2 copy.328
  576.9 10.9 fusion.16
  597.3 4.7 bitcast_convert_fusion.1
  601.9 6.6 copy.374
  608.5 5.0 reshape.449
  613.7 5.0 fusion.25
  618.7 6.1 copy.334
  624.8 4.3 convolution_multiply_fusion
  629.1 6.2 copy.333
  635.2 10.1 fusion.19
  646.6 2.8 bitcast_convert_fusion
  649.4 6.6 copy.376
  655.9 5.0 reshape.451
  661.2 3.9 fusion.35
  665.2 3.2 fusion.24
  668.4 5.3 copy.341
  678.2 6.2 copy.338
  696.8 3.1 convolution_add_fusion
  702.2 2.9 add_bitcast_fusion
  705.2 6.0 copy.380
  721.5 9.4 reduce-scatter.25.cloned.1.call-done
  735.4 8.1 reduce-scatter.27.cloned.1.call-done
  750.1 229.6 %all-reduce.17.cloned.1.call-done = (f32[3,768,384]{2,0,1:T(4,128)}, f32[2,768,384]{2,0,1:T(2,128)}) async-done(((f32[3,768,384]{2,0,1:T(4,128)}, f32[2,768,384]{2,0,1:T(2,128)}), (f32[3,768,384]{2,0,1:T(4,128)}, f32[2,768,384]{2,0,1:T(2,128)})) %all-reduce.17.cloned.1.call-update) | async-done | bytes 5898256
  983.0 125.3 %reduce-scatter.21.cloned.1.call-done = f32[48,384]{1,0:T(8,128)} async-done(((f32[768,384]{1,0:T(8,128)}), f32[48,384]{1,0:T(8,128)}) %reduce-scatter.21.cloned.1.call-update) | async-done | bytes 73744 | tf_op jit(solution)/shard_map/reduce_scatter | solution.py:130
  1108.3 128.6 %reduce-scatter.19.cloned.1.call-done = f32[48,384]{1,0:T(8,128)} async-done(((f32[768,384]{1,0:T(8,128)}), f32[48,384]{1,0:T(8,128)}) %reduce-scatter.19.cloned.1.call-update) | async-done | bytes 73744 | tf_op jit(solution)/shard_map/reduce_scatter | solution.py:128
  1236.8 128.6 %reduce-scatter.17.cloned.1.call-done = f32[48,384]{1,0:T(8,128)} async-done(((f32[768,384]{1,0:T(8,128)}), f32[48,384]{1,0:T(8,128)}) %reduce-scatter.17.cloned.1.call-update) | async-done | bytes 73744 | tf_op jit(solution)/shard_map/reduce_scatter | solution.py:127
  1365.5 142.6 %reduce-scatter.23.cloned.1.call-done = f32[48,1536]{1,0:T(8,128)} async-done(((f32[768,1536]{1,0:T(8,128)}), f32[48,1536]{1,0:T(8,128)}) %reduce-scatter.23.cloned.1.call-update) | async-done | bytes 294928 | tf_op jit(solution)/shard_map/reduce_scatter | solution.py:131
  1508.0 141.4 %reduce-scatter.31.cloned.1.call-done = f32[48,1536]{1,0:T(8,128)} async-done(((f32[768,1536]{1,0:T(8,128)}), f32[48,1536]{1,0:T(8,128)}) %reduce-scatter.31.cloned.1.call-update) | async-done | bytes 294928
  (562 shorter events, 278.5 us)
Async XLA Ops:
  7.2 48.7 %copy-start.4 = (bf16[2,4,64,768]{3,2,1,0:T(8,128)(2,1)S(1)}, bf16[2,4,64,768]{3,2,1,0:T(8,128)(2,1)}, u32[]{:S(2)}) copy-start(bf16[2,4,64,768]{3,2,1,0:T(8,128)(2,1)} %param.15) | copy-start | bytes 2359300
  7.2 47.3 %copy-start.128 = (s32[2,4]{1,0:T(2,128)S(1)}, s32[2,4]{1,0:T(2,128)}, u32[]{:S(2)}) copy-start(s32[2,4]{1,0:T(2,128)} %param.18) | copy-start | bytes 100
  7.2 47.9 %copy-start.129 = (s32[2,4,64]{2,1,0:T(4,128)S(1)}, s32[2,4,64]{2,1,0:T(4,128)}, u32[]{:S(2)}) copy-start(s32[2,4,64]{2,1,0:T(4,128)} %param.17) | copy-start | bytes 6148
  7.2 172.7 %all-gather.7.cloned.1.call-start = ((), (), s32[]{:S(2)}) async-start(), calls=%async_computation.9 | async-start | bytes 1253376 | tf_op jit(solution)/shard_map/all_gather | solution.py:116
  8.0 49.0 %copy-start.98 = (bf16[48,384]{1,0:T(8,128)(2,1)S(1)}, bf16[48,384]{1,0:T(8,128)(2,1)}, u32[]{:S(2)}) copy-start(bf16[48,384]{1,0:T(8,128)(2,1)} %param.22) | copy-start | bytes 110596
  8.0 181.1 %all-gather.5.cloned.1.call-start = ((), (), s32[]{:S(2)}) async-start(), calls=%async_computation.8 | async-start | bytes 1880064 | tf_op jit(solution)/shard_map/all_gather | solution.py:113
  8.7 239.7 %all-reduce.23.cloned.1.call-start = ((), (), s32[]{:S(2)}) async-start(), calls=%async_computation.22 | async-start | bytes 3145728 | tf_op jit(solution)/shard_map/psum | solution.py:137
  10.1 87.2 %copy-start.99 = (bf16[48,384]{1,0:T(8,128)(2,1)S(1)}, bf16[48,384]{1,0:T(8,128)(2,1)}, u32[]{:S(2)}) copy-start(bf16[48,384]{1,0:T(8,128)(2,1)} %param.23) | copy-start | bytes 110596
  10.1 130.1 %copy-start.100 = (bf16[48,384]{1,0:T(8,128)(2,1)S(1)}, bf16[48,384]{1,0:T(8,128)(2,1)}, u32[]{:S(2)}) copy-start(bf16[48,384]{1,0:T(8,128)(2,1)} %param.25) | copy-start | bytes 110596
  11.7 168.2 %copy-start.105 = (f32[256]{0:T(256)}, f32[256]{0:T(256)S(1)}, u32[]{:S(2)}) copy-start(f32[256]{0:T(256)S(1)} %div.157) | copy-start | bytes 3076
  11.7 168.1 %copy-start.107 = (f32[256]{0:T(256)}, f32[256]{0:T(256)S(1)}, u32[]{:S(2)}) copy-start(f32[256]{0:T(256)S(1)} %div.168) | copy-start | bytes 3076
  11.8 43.2 %copy-start.121 = (f32[256]{0:T(256)}, f32[256]{0:T(256)S(1)}, u32[]{:S(2)}) copy-start(f32[256]{0:T(256)S(1)} %add.389) | copy-start | bytes 3076
  11.8 168.0 %copy-start.111 = (f32[256]{0:T(256)}, f32[256]{0:T(256)S(1)}, u32[]{:S(2)}) copy-start(f32[256]{0:T(256)S(1)} %rsqrt.66) | copy-start | bytes 3076
  11.9 43.1 %copy-start.122 = (f32[256]{0:T(256)}, f32[256]{0:T(256)S(1)}, u32[]{:S(2)}) copy-start(f32[256]{0:T(256)S(1)} %add.434) | copy-start | bytes 3076
  11.9 167.9 %copy-start.113 = (f32[256]{0:T(256)}, f32[256]{0:T(256)S(1)}, u32[]{:S(2)}) copy-start(f32[256]{0:T(256)S(1)} %rsqrt.69) | copy-start | bytes 3076
  56.9 132.1 %copy-start.65 = (bf16[256,768]{1,0:T(8,128)(2,1)}, bf16[256,768]{1,0:T(8,128)(2,1)S(1)}, u32[]{:S(2)}) copy-start(bf16[256,768]{1,0:T(8,128)(2,1)S(1)} %get-tuple-element.120) | copy-start | bytes 1179652
  97.3 115.8 %copy-start.15 = (bf16[768,384]{1,0:T(8,128)(2,1)}, bf16[768,384]{1,0:T(8,128)(2,1)S(1)}, u32[]{:S(2)}) copy-start(bf16[768,384]{1,0:T(8,128)(2,1)S(1)} %all_gather.30) | copy-start | bytes 1769476
  140.2 112.0 %copy-start.20 = (bf16[768,384]{1,0:T(8,128)(2,1)}, bf16[768,384]{1,0:T(8,128)(2,1)S(1)}, u32[]{:S(2)}) copy-start(bf16[768,384]{1,0:T(8,128)(2,1)S(1)} %all_gather.32) | copy-start | bytes 1769476
  179.9 100.2 %copy-start.18 = (bf16[768,384]{1,0:T(8,128)(2,1)}, bf16[768,384]{1,0:T(8,128)(2,1)S(1)}, u32[]{:S(2)}) copy-start(bf16[768,384]{1,0:T(8,128)(2,1)S(1)} %all_gather.33) | copy-start | bytes 1769476
  206.1 6.9 copy-start.56
  214.4 150.7 %all-reduce.21.cloned.1.call-start = ((), (), s32[]{:S(2)}) async-start(), calls=%async_computation.21 | async-start | bytes 3145728 | tf_op jit(solution)/shard_map/psum | solution.py:137
  256.8 12.4 copy-start.39
  269.2 9.6 copy-start.59
  281.4 94.0 %all-gather.9.cloned.1.call-start = ((), (), s32[]{:S(2)}) async-start(), calls=%async_computation.10 | async-start | bytes 2506752 | tf_op jit(solution)/shard_map/all_gather | solution.py:119
  281.5 7.7 collective-permute-start.1
  282.9 11.1 collective-permute-start
  283.6 127.5 %all-reduce.29.cloned.1.call-start = ((), (), s32[]{:S(2)}) async-start(), calls=%async_computation.25 | async-start | bytes 1572864 | tf_op jit(solution)/shard_map/psum | solution.py:141
  289.2 7.4 collective-permute-start.3
  293.9 9.1 collective-permute-start.2
  296.6 10.1 collective-permute-start.5
  303.0 10.3 collective-permute-start.4
  306.7 10.1 collective-permute-start.7
  313.3 10.6 collective-permute-start.6
  316.8 8.8 collective-permute-start.9
  323.9 8.8 collective-permute-start.8
  325.6 9.7 collective-permute-start.11
  332.8 11.0 collective-permute-start.10
  335.3 17.9 %collective-permute-start.13 = (bf16[48,1536]{1,0:T(8,128)(2,1)S(1)}, bf16[48,1536]{1,0:T(8,128)(2,1)S(1)}, u32[]{:S(2)}, u32[]{:S(2)}) collective-permute-start(bf16[48,1536]{1,0:T(8,128)(2,1)S(1)} %collective-permute-done.11), channel_id=1, source_target_pairs={{0,30},{2,0},{4,2},{6,4},{8,6},{10,8},{12,10},{14,12},{16,14},{18,... | collective-permute-start | bytes 442376 | tf_op jit(solution)/shard_map/ppermute | solution.py:25
  343.8 8.7 collective-permute-start.12
  352.5 11.9 collective-permute-start.14
  375.4 6.4 copy-start.33
  395.8 40.0 %all-reduce.19.cloned.1.call-start = ((), (), s32[]{:S(2)}) async-start(), calls=%async_computation.20 | async-start | bytes 3145728 | tf_op jit(solution)/shard_map/psum | solution.py:137
  403.4 101.2 %all-reduce.27.cloned.1.call-start = ((), (), s32[]{:S(2)}) async-start(), calls=%async_computation.24 | async-start | bytes 1572864 | tf_op jit(solution)/shard_map/psum | solution.py:141
  435.8 5.6 copy-start.19
  484.1 104.9 %all-reduce.25.cloned.1.call-start = ((), (), s32[]{:S(2)}) async-start(), calls=%async_computation.23 | async-start | bytes 1572864 | tf_op jit(solution)/shard_map/psum | solution.py:141
  566.0 154.2 %reduce-scatter.29.cloned.1.call-start = ((), (), s32[]{:S(2)}) async-start(), calls=%async_computation.17 | async-start | bytes 417792
  576.9 10.9 copy-start.109
  576.9 11.5 copy-start.110
  588.9 5.3 copy-start.115
  597.2 133.7 %reduce-scatter.25.cloned.1.call-start = ((), (), s32[]{:S(2)}) async-start(), calls=%async_computation.15 | async-start | bytes 2654208
  613.5 130.1 %reduce-scatter.27.cloned.1.call-start = ((), (), s32[]{:S(2)}) async-start(), calls=%async_computation.16 | async-start | bytes 2654208
  635.2 11.3 copy-start.138
  660.9 318.8 %all-reduce.17.cloned.1.call-start = ((), (), s32[]{:S(2)}) async-start(), calls=%async_computation.19 | async-start | bytes 14155776
  684.5 423.8 %reduce-scatter.21.cloned.1.call-start = ((), (), s32[]{:S(2)}) async-start(), calls=%async_computation.13 | async-start | bytes 1253376 | tf_op jit(solution)/shard_map/reduce_scatter | solution.py:130
  687.6 549.3 %reduce-scatter.19.cloned.1.call-start = ((), (), s32[]{:S(2)}) async-start(), calls=%async_computation.12 | async-start | bytes 1253376 | tf_op jit(solution)/shard_map/reduce_scatter | solution.py:128
  691.5 673.9 %reduce-scatter.17.cloned.1.call-start = ((), (), s32[]{:S(2)}) async-start(), calls=%async_computation.11 | async-start | bytes 1253376 | tf_op jit(solution)/shard_map/reduce_scatter | solution.py:127
  694.5 813.5 %reduce-scatter.23.cloned.1.call-start = ((), (), s32[]{:S(2)}) async-start(), calls=%async_computation.14 | async-start | bytes 5013504 | tf_op jit(solution)/shard_map/reduce_scatter | solution.py:131
  700.0 949.4 %reduce-scatter.31.cloned.1.call-start = ((), (), s32[]{:S(2)}) async-start(), calls=%async_computation.18 | async-start | bytes 5013504
  711.2 5.4 copy-start.106
  711.2 5.4 copy-start.108
  711.2 5.4 copy-start.112
  711.3 5.4 copy-start.25
  711.3 5.4 copy-start.52
  711.3 5.4 copy-start.54
  (110 other events, 278.3 us)
Sparse Core Ops, SparseCore 0:
  10.7 59.4 all-gather.6
  72.9 61.6 all-gather.4
  214.5 17.3 all-reduce.22
  281.5 17.5 all-reduce.20
  301.8 68.1 all-gather.8
  395.9 15.1 all-reduce.28
  414.2 21.6 all-reduce.18
  484.2 20.4 all-reduce.26
  566.1 20.4 all-reduce.24
  597.3 122.7 reduce-scatter.28
  722.5 8.3 reduce-scatter.24
  733.0 10.4 reduce-scatter.26
  751.1 228.5 all-reduce.16
  985.6 122.6 reduce-scatter.20
  1114.2 122.6 reduce-scatter.18
  1242.7 122.6 reduce-scatter.16
  1371.9 136.1 reduce-scatter.22
  1513.6 135.7 reduce-scatter.30
